TPU v7x, 128 devices: a whole 4x4x4 slice. The times are simulated.
128 devices in a mesh: row: 8 (over z_hi, y), col: 16 (over x, z_lo, core).
Axes of the slice: x: 4, y: 4, z: 4 (z_hi: 2, z_lo: 2; z = z_hi * 2 + z_lo), core: 2. Of those that a mesh axis runs over, the one named last changes fastest.
Arguments:
- features: bfloat16 [16, 8192, 128], P('col', 'row'), may hold values from 0.099609375 to 3
- relu_mask: int32 [16, 8192, 128], P('col', 'row'), may hold values 0 or 1
- tiles: bfloat16 [8, 16, 184, 256, 256], P('row', 'col'), may hold values from -0.25 to 0.25
- tile_rows: int32 [8, 16, 184], P('row', 'col'), may hold values from 0 to 63, as said below
- tile_cols: int32 [8, 16, 184], P('row', 'col'), may hold values from 0 to 31
- tile_count: int32 [8, 16], P('row', 'col'), may hold values from 23 to 184, as said below
- weight: bfloat16 [128, 128], replicated, may hold values from -0.5 to 0.5
- cotangent: bfloat16 [8, 16384, 128], P('row', 'col'), may hold values from -6 to 6
Outputs:
- out_pre: bfloat16 [8, 16384, 128], P('row', 'col')
- weight_grad: float32 [128, 128], replicated
- input_grad: bfloat16 [16, 8192, 128], P('col', 'row')
Inputs may be any that keep to these rules, and one draw needn't show every extreme that they name: `tile_rows`: within one panel pair the live and dead slots name distinct (block row, block column) pairs. `tile_count`: counts differ widely between panel pairs.
All inputs are finite; a program needn't handle non-finite values. No bound on the sum of `relu_mask` on one device may be relied on, other than what follows from the above.
Results may differ from a plain program's by a relative error of at most 0.022.
Values may be sent and summed in bfloat16 or wider, within the bound.
A program may use at most 192 MiB of HBM per device.

v0:
```python
import jax
import jax.numpy as jnp
from jax import lax
from jax.sharding import PartitionSpec as P


def slot_products(tile_vals, row_ids, col_ids, source, backward):
    tile_size = tile_vals.shape[1]
    feature_width = source.shape[1]
    if backward:
        blocks = source.reshape(-1, tile_size, feature_width)[row_ids]
        products = jnp.einsum("sij,sif->sjf", tile_vals, blocks, preferred_element_type=jnp.float32)
        target_ids = col_ids
    else:
        blocks = source.reshape(-1, tile_size, feature_width)[col_ids]
        products = jnp.einsum("sij,sjf->sif", tile_vals, blocks, preferred_element_type=jnp.float32)
        target_ids = row_ids
    return (products, target_ids)


def apply_tiles(tile_vals, row_ids, col_ids, live_count, source, backward, segments):
    feature_width = source.shape[1]
    slots = tile_vals.shape[0]
    products, target_ids = slot_products(tile_vals, row_ids, col_ids, source, backward)
    live_slots = jnp.arange(slots, dtype=jnp.int32) < live_count
    targets = jnp.arange(segments, dtype=jnp.int32)[:, None] == target_ids[None, :]
    selector = jnp.where(targets & live_slots[None, :], 1.0, 0.0).astype(jnp.float32)
    total = jnp.einsum(
        "rs,sif->rif",
        selector,
        products,
        precision=lax.Precision.HIGHEST,
        preferred_element_type=jnp.float32,
    )
    return total.reshape(-1, feature_width)


def body(features, relu_mask, tiles, tile_rows, tile_cols, tile_count, weight, cotangent):
    tile_size = tiles.shape[3]
    mask_rows = relu_mask[0]
    hidden = features[0] * mask_rows.astype(jnp.bfloat16)
    tile_vals = tiles[0, 0]
    row_ids = tile_rows[0, 0]
    col_ids = tile_cols[0, 0]
    live_count = tile_count[0, 0]
    own_rows = hidden.shape[0]
    row_blocks = own_rows * lax.axis_size("col") // tile_size
    col_blocks = own_rows * lax.axis_size("row") // tile_size
    feat_panel = lax.all_gather(hidden, "row", axis=0, tiled=True)
    forward_terms = apply_tiles(
        tile_vals, row_ids, col_ids, live_count, feat_panel, False, row_blocks
    )
    forward_terms = lax.optimization_barrier(forward_terms.astype(jnp.bfloat16)).astype(jnp.float32)
    aggregate = lax.psum_scatter(
        forward_terms.astype(jnp.bfloat16), "col", scatter_dimension=0, tiled=True
    )
    out_pre = jnp.dot(aggregate, weight, preferred_element_type=jnp.float32).astype(jnp.bfloat16)
    cot_rows = cotangent[0]
    weight_term = lax.dot_general(
        aggregate, cot_rows, (((0,), (0,)), ((), ())), preferred_element_type=jnp.float32
    )
    grad_scale = 1.0 / jnp.sqrt(jnp.float32(own_rows * lax.axis_size("row") * lax.axis_size("col")))
    weight_grad = lax.psum(weight_term, ("row", "col")) * grad_scale
    grad_rows = lax.dot_general(
        cot_rows, weight, (((1,), (1,)), ((), ())), preferred_element_type=jnp.float32
    )
    grad_rows = lax.all_gather(grad_rows.astype(jnp.bfloat16), "col", axis=0, tiled=True)
    back_terms = apply_tiles(tile_vals, row_ids, col_ids, live_count, grad_rows, True, col_blocks)
    back_terms = lax.optimization_barrier(back_terms.astype(jnp.bfloat16)).astype(jnp.float32)
    summed = lax.psum_scatter(
        back_terms.astype(jnp.bfloat16), "row", scatter_dimension=0, tiled=True
    ).astype(jnp.float32)
    input_grad = (summed * mask_rows.astype(jnp.float32)).astype(jnp.bfloat16)
    return (out_pre[None], weight_grad, input_grad[None])


def solution(mesh):
    placed = (
        P("col", "row", None),
        P("col", "row", None),
        P("row", "col", None, None, None),
        P("row", "col", None),
        P("row", "col", None),
        P("row", "col"),
        P(),
        P("row", "col", None),
    )
    return jax.shard_map(
        body,
        mesh=mesh,
        in_specs=placed,
        out_specs=(P("row", "col", None), P(), P("col", "row", None)),
        check_vma=False,
    )
```

profile of v0, /device:TPU:1, one launch (start us, length us, event | category | flops | bytes accessed | tf_op | source)
XLA Modules:
  0.0 451.2 jit_solution(6644754055595961643)
XLA Ops:
  7.2 0.0 copy-start
  7.2 0.0 all-gather.6.cloned.1.call-start
  7.2 1.9 convert_multiply_fusion
  9.1 0.0 all-gather.6.cloned.1.call-update
  9.1 0.0 all-gather.4.cloned.1.call-start
  9.2 0.0 copy-done
  9.2 1.7 convolution_convert_fusion
  10.9 0.0 all-gather.4.cloned.1.call-update
  10.9 0.0 reduce-scatter.3.cloned.1.call-start
  11.6 0.7 compare_select_fusion.1
  12.3 55.5 %all-gather.6.cloned.1.call-done = bf16[1,8192,128]{2,1,0:T(8,128)(2,1)} async-done(((bf16[1,1024,128]{2,1,0:T(8,128)(2,1)}), bf16[1,8192,128]{2,1,0:T(8,128)(2,1)}) %all-gather.6.cloned.1.call-update) | async-done | bytes 2097168 | tf_op jit(solution)/shard_map/all_gather | solution.py:49
  67.9 9.7 %gather_fusion = bf16[184,256,128]{2,1,0:T(8,128)(2,1)} fusion(bf16[32,256,128]{2,1,0:T(8,128)(2,1)} %bitcast.56, s32[1024]{0:T(1024)S(1)} %pad_clamp_fusion.1), kind=kCustom, calls=%fused_computation | custom fusion | bytes 24117984 | tf_op jit(solution)/shard_map/gather | solution.py:15
  77.5 21.6 %fusion.6 = f32[184,128,256]{2,1,0:T(8,128)} fusion(bf16[184,256,128]{2,1,0:T(8,128)(2,1)} %gather_fusion, bf16[1,1,184,256,256]{4,3,2,1,0:T(8,128)(2,1)} %param.10), kind=kOutput, calls=%fused_computation.8 | convolution fusion | flops 3087007744 | bytes 60293120 | tf_op jit(solution)/shard_map/sij,sjf->sif/dot_general | solution.py:16
  99.1 0.0 copy-start.3
  99.1 24.6 %copy.13 = f32[184,128,256]{1,0,2:T(8,128)} copy(f32[184,128,256]{2,1,0:T(8,128)} %fusion.6) | data formatting | bytes 48234496 | tf_op jit(solution)/shard_map/sij,sjf->sif/dot_general | solution.py:16
  123.7 0.0 copy-done.3
  123.7 20.8 %fusion.8 = bf16[64,256,128]{2,0,1:T(8,128)(2,1)S(1)} fusion(f32[184,128,256]{1,0,2:T(8,128)} %copy.13, s32[184]{0:T(256)S(1)} %bitcast.60, pred[184]{0:T(512)(128)(4,1)S(1)} %iota_compare_fusion.2), kind=kOutput, calls=%fused_computation.10 | convolution fusion | flops 4632644096 | bytes 28312472 | tf_op jit(solution)/shard_map/rs,sif->rif/dot_general | solution.py:28
  144.5 4.7 %copy.11 = bf16[64,256,128]{2,1,0:T(8,128)(2,1)} copy(bf16[64,256,128]{2,0,1:T(8,128)(2,1)S(1)} %fusion.8) | data formatting | bytes 8388608 | tf_op jit(solution)/shard_map/convert_element_type | solution.py:53
  149.1 0.0 reduce-scatter.3.cloned.1.call-update
  149.2 0.0 reduce-scatter.5.cloned.1.call-start
  149.2 0.0 all-gather.4.cloned.1.call-done
  149.3 10.3 %gather_fusion.1 = bf16[184,256,128]{2,1,0:T(8,128)(2,1)} fusion(bf16[64,256,128]{2,1,0:T(8,128)(2,1)} %bitcast.57, s32[1024]{0:T(1024)S(1)} %pad_clamp_fusion), kind=kCustom, calls=%fused_computation.1 | custom fusion | bytes 24117984 | tf_op jit(solution)/shard_map/gather | solution.py:11
  159.5 22.0 %fusion.4 = f32[184,128,256]{2,1,0:T(8,128)} fusion(bf16[184,256,128]{2,1,0:T(8,128)(2,1)} %gather_fusion.1, bf16[1,1,184,256,256]{4,3,2,1,0:T(8,128)(2,1)} %param.10), kind=kOutput, calls=%fused_computation.6 | convolution fusion | flops 3087007744 | bytes 60293120 | tf_op jit(solution)/shard_map/sij,sif->sjf/dot_general | solution.py:12
  181.6 0.0 copy-start.4
  181.6 24.6 %copy.14 = f32[184,128,256]{1,0,2:T(8,128)} copy(f32[184,128,256]{2,1,0:T(8,128)} %fusion.4) | data formatting | bytes 48234496 | tf_op jit(solution)/shard_map/sij,sif->sjf/dot_general | solution.py:12
  206.2 0.0 copy-done.4
  206.2 0.0 copy-start.2
  206.2 0.0 copy-start.1
  206.2 17.1 %fusion.11 = bf16[32,256,128]{2,0,1:T(8,128)(2,1)S(1)} fusion(f32[184,128,256]{1,0,2:T(8,128)} %copy.14, s32[184]{0:T(256)S(1)} %bitcast.61, pred[184]{0:T(512)(128)(4,1)S(1)} %iota_compare_fusion.2), kind=kOutput, calls=%fused_computation.11 | convolution fusion | flops 2316322048 | bytes 26215320 | tf_op jit(solution)/shard_map/rs,sif->rif/dot_general | solution.py:28
  223.3 2.1 copy.12
  225.4 0.0 reduce-scatter.5.cloned.1.call-update
  225.4 0.0 all-reduce.2.cloned.1.call-start
  225.5 0.0 reduce-scatter.3.cloned.1.call-done
  225.5 1.9 fusion.18
  227.4 0.0 all-reduce.2.cloned.1.call-update
  227.4 0.0 copy-done.2
  227.4 1.9 fusion.14
  229.3 70.3 %reduce-scatter.5.cloned.1.call-done = bf16[1024,128]{1,0:T(8,128)(2,1)} async-done(((bf16[8192,128]{1,0:T(8,128)(2,1)}), bf16[1024,128]{1,0:T(8,128)(2,1)}) %reduce-scatter.5.cloned.1.call-update) | async-done | bytes 262160 | tf_op jit(solution)/shard_map/reduce_scatter | solution.py:70
  299.6 0.0 copy-done.1
  299.6 1.7 fusion.16
  301.3 141.9 %all-reduce.2.cloned.1.call-done = f32[128,128]{1,0:T(8,128)} async-done(((f32[128,128]{1,0:T(8,128)}), f32[128,128]{1,0:T(8,128)}) %all-reduce.2.cloned.1.call-update) | async-done | bytes 65552 | tf_op jit(solution)/shard_map/psum | solution.py:63
  443.2 1.5 broadcast_multiply_fusion
  (4 shorter events, 0.0 us)
Async XLA Ops:
  7.2 2.0 copy-start
  7.2 60.7 %all-gather.6.cloned.1.call-start = ((), (), s32[]{:S(2)}) async-start(), calls=%async_computation.6 | async-start | bytes 2359296 | tf_op jit(solution)/shard_map/all_gather | solution.py:49
  9.1 140.1 %all-gather.4.cloned.1.call-start = ((), (), s32[]{:S(2)}) async-start(), calls=%async_computation.4 | async-start | bytes 4456448 | tf_op jit(solution)/shard_map/all_gather | solution.py:67
  10.9 214.6 %reduce-scatter.3.cloned.1.call-start = ((), (), s32[]{:S(2)}) async-start(), calls=%async_computation.2 | async-start | bytes 4456448 | tf_op jit(solution)/shard_map/reduce_scatter | solution.py:54
  99.1 24.6 %copy-start.3 = (s32[1,1,184]{2,1,0:T(1,128)S(1)}, s32[1,1,184]{2,1,0:T(1,128)}, u32[]{:S(2)}) copy-start(s32[1,1,184]{2,1,0:T(1,128)} %param.11) | copy-start | bytes 2212
  149.2 150.4 %reduce-scatter.5.cloned.1.call-start = ((), (), s32[]{:S(2)}) async-start(), calls=%async_computation.5 | async-start | bytes 2359296 | tf_op jit(solution)/shard_map/reduce_scatter | solution.py:70
  181.6 24.6 %copy-start.4 = (s32[1,1,184]{2,1,0:T(1,128)S(1)}, s32[1,1,184]{2,1,0:T(1,128)}, u32[]{:S(2)}) copy-start(s32[1,1,184]{2,1,0:T(1,128)} %param.12) | copy-start | bytes 2212
  206.2 21.2 %copy-start.2 = (bf16[128,128]{1,0:T(8,128)(2,1)S(1)}, bf16[128,128]{1,0:T(8,128)(2,1)}, u32[]{:S(2)}) copy-start(bf16[128,128]{1,0:T(8,128)(2,1)} %param.14) | copy-start | bytes 98308
  206.2 93.4 %copy-start.1 = (s32[1,1024,128]{2,1,0:T(8,128)S(1)}, s32[1,1024,128]{2,1,0:T(8,128)}, u32[]{:S(2)}) copy-start(s32[1,1024,128]{2,1,0:T(8,128)} %param.9) | copy-start | bytes 1572868
  225.4 217.8 %all-reduce.2.cloned.1.call-start = ((), (), s32[]{:S(2)}) async-start(), calls=%async_computation.3 | async-start | bytes 131072 | tf_op jit(solution)/shard_map/psum | solution.py:63
Sparse Core Ops, SparseCore 0:
  10.9 56.9 all-gather.5
  70.1 37.8 all-gather.3
  149.3 63.9 reduce-scatter.2
  225.6 74.0 reduce-scatter.4
  305.5 137.6 all-reduce.1
where the time goes:
time: 452 us; the launch traced here: 451 us
  waiting for transfers between devices  268 us (59%)
  matrix products  86.9 us (19%)
  local copies, waits for them, and re-layouts  75.9 us (17%)
  between operations  14.5 us (3%)
  other arithmetic  5.8 us (1%)
    psum x1, waiting for transfers between devices, body(): weight_grad = lax.psum(weight_term, ('row', 'col')) * grad_scale  142 us
    reduce_scatter x1, waiting for transfers between devices, body(): lax.psum_scatter(back_terms.astype(jnp.bfloat16), 'row', scatter_dimensio...  70.3 us
    all_gather x1, waiting for transfers between devices, body(): feat_panel = lax.all_gather(hidden, 'row', axis=0, tiled=True)  55.5 us
    dot_general x2, matrix products, apply_tiles(): jnp.einsum('rs,sif->rif', selector, products, precision=lax.Precision.HIG...  37.8 us
    dot_general x1, local copies, waits for them, and re-layouts, slot_products(): jnp.einsum('sij,sif->sjf', tile_vals, blocks, preferred_element_type=jnp....  24.6 us
    dot_general x1, local copies, waits for them, and re-layouts, slot_products(): jnp.einsum('sij,sjf->sif', tile_vals, blocks, preferred_element_type=jnp....  24.6 us
    dot_general x1, matrix products, slot_products(): jnp.einsum('sij,sif->sjf', tile_vals, blocks, preferred_element_type=jnp....  22 us
    dot_general x1, matrix products, slot_products(): jnp.einsum('sij,sjf->sif', tile_vals, blocks, preferred_element_type=jnp....  21.6 us
  transfers between devices with their start and end apart: 5, of which 3 were waited for; matrix products, arithmetic and copies ran while one was open for 37% of the time, Pallas kernels for 0%

commit v1 on v0

--- a/solution.py
+++ b/solution.py
@@ -1,7 +1,17 @@
+import functools
 import jax
 import jax.numpy as jnp
 from jax import lax
 from jax.sharding import PartitionSpec as P
+
+
+def settle_bars(mine, peer_axis):
+    passed = lax.all_gather(mine, axis_name=peer_axis)
+    all_rows = jnp.sum(passed, axis=0)
+    return all_rows
+
+
+guide_the_strips_all = functools.partial(settle_bars, peer_axis=("row", "col"))
 
 
 def slot_products(tile_vals, row_ids, col_ids, source, backward):
@@ -60,7 +70,7 @@
         aggregate, cot_rows, (((0,), (0,)), ((), ())), preferred_element_type=jnp.float32
     )
     grad_scale = 1.0 / jnp.sqrt(jnp.float32(own_rows * lax.axis_size("row") * lax.axis_size("col")))
-    weight_grad = lax.psum(weight_term, ("row", "col")) * grad_scale
+    weight_grad = guide_the_strips_all(weight_term) * grad_scale
     grad_rows = lax.dot_general(
         cot_rows, weight, (((1,), (1,)), ((), ())), preferred_element_type=jnp.float32
     )

time: 452 us -> 517 us (1.14)
  waiting for transfers between devices: 268 us -> 329 us
    all_gather x0 -> x1, waiting for transfers between devices: none -> 203 us  [settle_bars(): passed = lax.all_gather(mine, axis_name=peer_axis)]
    psum x1 -> x0, waiting for transfers between devices: 142 us -> none  [body(): weight_grad = lax.psum(weight_term, ('row', 'col')) * grad_scale]
  transfers between devices with their start and end apart: 5 -> 5, of which waited for: 3 -> 3; matrix products, arithmetic and copies ran while one was open for 37% -> 32% of each run, Pallas kernels for 0% -> 0%
where the time goes in v1:
time: 517 us; the launch traced here: 516 us
  waiting for transfers between devices  329 us (64%)
  matrix products  86.9 us (17%)
  local copies, waits for them, and re-layouts  76 us (15%)
  between operations  14.5 us (3%)
  other arithmetic  8.77 us (2%)
    all_gather x1, waiting for transfers between devices, settle_bars(): passed = lax.all_gather(mine, axis_name=peer_axis)  203 us
    reduce_scatter x1, waiting for transfers between devices, body(): lax.psum_scatter(back_terms.astype(jnp.bfloat16), 'row', scatter_dimensio...  70.3 us
    all_gather x1, waiting for transfers between devices, body(): feat_panel = lax.all_gather(hidden, 'row', axis=0, tiled=True)  55.5 us
    dot_general x2, matrix products, apply_tiles(): jnp.einsum('rs,sif->rif', selector, products, precision=lax.Precision.HIG...  37.8 us
    dot_general x1, local copies, waits for them, and re-layouts, slot_products(): jnp.einsum('sij,sif->sjf', tile_vals, blocks, preferred_element_type=jnp....  24.6 us
    dot_general x1, local copies, waits for them, and re-layouts, slot_products(): jnp.einsum('sij,sjf->sif', tile_vals, blocks, preferred_element_type=jnp....  24.6 us
    dot_general x1, matrix products, slot_products(): jnp.einsum('sij,sif->sjf', tile_vals, blocks, preferred_element_type=jnp....  22 us
    dot_general x1, matrix products, slot_products(): jnp.einsum('sij,sjf->sif', tile_vals, blocks, preferred_element_type=jnp....  21.6 us
  transfers between devices with their start and end apart: 5, of which 3 were waited for; matrix products, arithmetic and copies ran while one was open for 32% of the time, Pallas kernels for 0%

profile of v1, /device:TPU:1, one launch (start us, length us, event | category | flops | bytes accessed | tf_op | source)
XLA Modules:
  0.0 515.7 jit_solution(16565796133954381582)
XLA Ops:
  7.2 0.0 copy-start
  7.2 0.0 all-gather.8.cloned.1.call-start
  7.2 1.9 convert_multiply_fusion
  9.1 0.0 all-gather.8.cloned.1.call-update
  9.1 0.0 all-gather.6.cloned.1.call-start
  9.2 0.0 copy-done
  9.2 1.7 convolution_convert_fusion
  10.9 0.0 all-gather.6.cloned.1.call-update
  10.9 0.0 reduce-scatter.3.cloned.1.call-start
  11.6 0.7 compare_select_fusion.1
  12.3 55.5 %all-gather.8.cloned.1.call-done = bf16[1,8192,128]{2,1,0:T(8,128)(2,1)} async-done(((bf16[1,1024,128]{2,1,0:T(8,128)(2,1)}), bf16[1,8192,128]{2,1,0:T(8,128)(2,1)}) %all-gather.8.cloned.1.call-update) | async-done | bytes 2097168 | tf_op jit(solution)/shard_map/all_gather | solution.py:59
  67.9 9.7 %gather_fusion = bf16[184,256,128]{2,1,0:T(8,128)(2,1)} fusion(bf16[32,256,128]{2,1,0:T(8,128)(2,1)} %bitcast.57, s32[1024]{0:T(1024)S(1)} %pad_clamp_fusion.1), kind=kCustom, calls=%fused_computation | custom fusion | bytes 24117984 | tf_op jit(solution)/shard_map/gather | solution.py:25
  77.5 21.6 %fusion.6 = f32[184,128,256]{2,1,0:T(8,128)} fusion(bf16[184,256,128]{2,1,0:T(8,128)(2,1)} %gather_fusion, bf16[1,1,184,256,256]{4,3,2,1,0:T(8,128)(2,1)} %param.10), kind=kOutput, calls=%fused_computation.8 | convolution fusion | flops 3087007744 | bytes 60293120 | tf_op jit(solution)/shard_map/sij,sjf->sif/dot_general | solution.py:26
  99.1 0.0 copy-start.3
  99.1 24.6 %copy.13 = f32[184,128,256]{1,0,2:T(8,128)} copy(f32[184,128,256]{2,1,0:T(8,128)} %fusion.6) | data formatting | bytes 48234496 | tf_op jit(solution)/shard_map/sij,sjf->sif/dot_general | solution.py:26
  123.7 0.0 copy-done.3
  123.7 20.8 %fusion.8 = bf16[64,256,128]{2,0,1:T(8,128)(2,1)S(1)} fusion(f32[184,128,256]{1,0,2:T(8,128)} %copy.13, s32[184]{0:T(256)S(1)} %bitcast.62, pred[184]{0:T(512)(128)(4,1)S(1)} %iota_compare_fusion.2), kind=kOutput, calls=%fused_computation.10 | convolution fusion | flops 4632644096 | bytes 28312472 | tf_op jit(solution)/shard_map/rs,sif->rif/dot_general | solution.py:38
  144.5 4.7 copy.11
  149.1 0.0 reduce-scatter.3.cloned.1.call-update
  149.2 0.0 reduce-scatter.5.cloned.1.call-start
  149.2 0.0 all-gather.6.cloned.1.call-done
  149.3 10.3 %gather_fusion.1 = bf16[184,256,128]{2,1,0:T(8,128)(2,1)} fusion(bf16[64,256,128]{2,1,0:T(8,128)(2,1)} %bitcast.58, s32[1024]{0:T(1024)S(1)} %pad_clamp_fusion), kind=kCustom, calls=%fused_computation.1 | custom fusion | bytes 24117984 | tf_op jit(solution)/shard_map/gather | solution.py:21
  159.5 22.0 %fusion.4 = f32[184,128,256]{2,1,0:T(8,128)} fusion(bf16[184,256,128]{2,1,0:T(8,128)(2,1)} %gather_fusion.1, bf16[1,1,184,256,256]{4,3,2,1,0:T(8,128)(2,1)} %param.10), kind=kOutput, calls=%fused_computation.6 | convolution fusion | flops 3087007744 | bytes 60293120 | tf_op jit(solution)/shard_map/sij,sif->sjf/dot_general | solution.py:22
  181.6 0.0 copy-start.4
  181.6 24.6 %copy.14 = f32[184,128,256]{1,0,2:T(8,128)} copy(f32[184,128,256]{2,1,0:T(8,128)} %fusion.4) | data formatting | bytes 48234496 | tf_op jit(solution)/shard_map/sij,sif->sjf/dot_general | solution.py:22
  206.2 0.0 copy-done.4
  206.2 0.0 copy-start.2
  206.2 0.0 copy-start.1
  206.2 17.1 %fusion.11 = bf16[32,256,128]{2,0,1:T(8,128)(2,1)S(1)} fusion(f32[184,128,256]{1,0,2:T(8,128)} %copy.14, s32[184]{0:T(256)S(1)} %bitcast.63, pred[184]{0:T(512)(128)(4,1)S(1)} %iota_compare_fusion.2), kind=kOutput, calls=%fused_computation.11 | convolution fusion | flops 2316322048 | bytes 26215320 | tf_op jit(solution)/shard_map/rs,sif->rif/dot_general | solution.py:38
  223.3 2.2 copy.12
  225.5 0.0 reduce-scatter.5.cloned.1.call-update
  225.5 0.0 all-gather.10.cloned.1.call-start
  225.5 0.0 reduce-scatter.3.cloned.1.call-done
  225.6 1.9 fusion.18
  227.4 0.0 all-gather.10.cloned.1.call-update
  227.4 0.0 copy-done.2
  227.4 1.9 fusion.14
  229.3 70.3 %reduce-scatter.5.cloned.1.call-done = bf16[1024,128]{1,0:T(8,128)(2,1)} async-done(((bf16[8192,128]{1,0:T(8,128)(2,1)}), bf16[1024,128]{1,0:T(8,128)(2,1)}) %reduce-scatter.5.cloned.1.call-update) | async-done | bytes 262160 | tf_op jit(solution)/shard_map/reduce_scatter | solution.py:80
  299.6 0.0 copy-done.1
  299.7 1.7 fusion.16
  301.4 203.3 %all-gather.10.cloned.1.call-done = f32[16384,128]{1,0:T(8,128)} async-done(((f32[128,128]{1,0:T(8,128)}), f32[16384,128]{1,0:T(8,128)}) %all-gather.10.cloned.1.call-update) | async-done | bytes 8388624 | tf_op jit(solution)/shard_map/all_gather | solution.py:9
  504.7 3.8 reduce_sum.9
  508.5 0.6 broadcast_multiply_fusion
  (4 shorter events, 0.0 us)
Async XLA Ops:
  7.2 2.0 copy-start
  7.2 60.7 %all-gather.8.cloned.1.call-start = ((), (), s32[]{:S(2)}) async-start(), calls=%async_computation.5 | async-start | bytes 2359296 | tf_op jit(solution)/shard_map/all_gather | solution.py:59
  9.1 140.1 %all-gather.6.cloned.1.call-start = ((), (), s32[]{:S(2)}) async-start(), calls=%async_computation.3 | async-start | bytes 4456448 | tf_op jit(solution)/shard_map/all_gather | solution.py:77
  10.9 214.6 %reduce-scatter.3.cloned.1.call-start = ((), (), s32[]{:S(2)}) async-start(), calls=%async_computation.2 | async-start | bytes 4456448 | tf_op jit(solution)/shard_map/reduce_scatter | solution.py:64
  99.1 24.6 %copy-start.3 = (s32[1,1,184]{2,1,0:T(1,128)S(1)}, s32[1,1,184]{2,1,0:T(1,128)}, u32[]{:S(2)}) copy-start(s32[1,1,184]{2,1,0:T(1,128)} %param.11) | copy-start | bytes 2212
  149.2 150.5 %reduce-scatter.5.cloned.1.call-start = ((), (), s32[]{:S(2)}) async-start(), calls=%async_computation.4 | async-start | bytes 2359296 | tf_op jit(solution)/shard_map/reduce_scatter | solution.py:80
  181.6 24.6 %copy-start.4 = (s32[1,1,184]{2,1,0:T(1,128)S(1)}, s32[1,1,184]{2,1,0:T(1,128)}, u32[]{:S(2)}) copy-start(s32[1,1,184]{2,1,0:T(1,128)} %param.12) | copy-start | bytes 2212
  206.2 21.2 %copy-start.2 = (bf16[128,128]{1,0:T(8,128)(2,1)S(1)}, bf16[128,128]{1,0:T(8,128)(2,1)}, u32[]{:S(2)}) copy-start(bf16[128,128]{1,0:T(8,128)(2,1)} %param.14) | copy-start | bytes 98308
  206.2 93.5 %copy-start.1 = (s32[1,1024,128]{2,1,0:T(8,128)S(1)}, s32[1,1024,128]{2,1,0:T(8,128)}, u32[]{:S(2)}) copy-start(s32[1,1024,128]{2,1,0:T(8,128)} %param.9) | copy-start | bytes 1572868
  225.5 279.2 %all-gather.10.cloned.1.call-start = ((), (), s32[]{:S(2)}) async-start(), calls=%async_computation.6 | async-start | bytes 8454144 | tf_op jit(solution)/shard_map/all_gather | solution.py:9
Sparse Core Ops, SparseCore 0:
  10.9 56.9 all-gather.7
  70.1 37.8 all-gather.5
  149.3 63.9 reduce-scatter.2
  225.6 74.0 reduce-scatter.4
  301.9 202.7 all-gather.9
